TPU v7x, 32 devices: a whole 2x2x4 slice. The times are simulated.
32 devices in a mesh: tile: 8 (over y, x, core), epoch: 4 (over z).
Axes of the slice: x: 2, y: 2, z: 4, core: 2. Of those that a mesh axis runs over, the one named last changes fastest.
Arguments:
- residual: bfloat16 [8, 128, 64, 128], P('tile', 'epoch'), may hold values from -6 to 6
- inv_variance: float32 [8, 128, 64, 128], P('tile', 'epoch'), may hold values from 0.25 to 4
- psf_coeff: float32 [8, 128, 16], P('tile', 'epoch'), may hold values from -5 to 5
- psf_taps: float32 [16, 2, 25], replicated, may hold values from -1.25 to 1.25
- patch_owner: int32 [8, 128, 1], P('tile', 'epoch'), may hold values from 0 to 3; in each aligned block of 32 rows (0 to 31, 32 to 63, ..., all dimensions but the last counted through in order) at most 16 rows name the same one
- patch_slot: int32 [8, 128], P('tile', 'epoch'), may hold values from 0 to 7
- band_id: int32 [8, 128], P('tile', 'epoch'), may hold values from 0 to 5
- tile_offset: int32 [8, 128], P('tile', 'epoch'), may hold values from 0 to 2
- col_shift: int32 [8, 128], P('tile', 'epoch'), may hold values from 0 to 7
Outputs:
- scene_adjoint: float32 [8, 6, 32, 64, 128], P('tile', None, 'epoch')
Inputs may be any that keep to these rules, and one draw needn't show every extreme that they name: Among the 32 blocks of one device at most 16 have the same patch_owner, and in every draw some owner receives exactly 16 from some device.
All inputs are finite; a program needn't handle non-finite values.
Results may differ from a plain program's by a relative error of at most 0.0003.
Values sent between devices are 32-bit elements; how exact they have to be, the bound alone decides.
No kernel may reach another device: no remote copies, remote signals or barrier semaphores. Data moves between devices by JAX's collectives and lax.ppermute only.
A program may use at most 64 MiB of HBM per device.

v0:
```python
import functools

import jax
import jax.numpy as jnp
from jax import lax
from jax.experimental import pallas as pl
from jax.experimental.pallas import tpu as pltpu
from jax.sharding import PartitionSpec as P


BANDS = 6
PATCHES = 32
HEAD = 8
LANES = 128


SMEM = pltpu.SMEM
VMEM = pltpu.VMEM
MIB = 1 << 20


def halves(x):
    high = x.astype(jnp.bfloat16)
    low = (x - high.astype(jnp.float32)).astype(jnp.bfloat16)
    return high, low


def plan_chunks(capacity):
    if capacity >= 16:
        sizes = (capacity // 4, capacity // 2, capacity - capacity // 4 - capacity // 2)
    else:
        sizes = (capacity // 2, capacity - capacity // 2)
    starts = [sum(sizes[:k]) for k in range(len(sizes))]
    return list(zip(starts, sizes))


def head_lanes():
    return lax.broadcasted_iota(jnp.int32, (HEAD, LANES), 1)


def build_bands(taps_ref, cols_ref, rows_ref):
    comps, _, taps = taps_ref.shape
    cols = cols_ref.shape[1] // 2
    rows = rows_ref.shape[1] // 4
    half = (taps - 1) // 2
    tap = lax.broadcasted_iota(jnp.int32, (taps, LANES), 0)
    lane = lax.broadcasted_iota(jnp.int32, (taps, LANES), 1)
    place_col = (lax.rem(lane + tap - half + cols, cols) == 0).astype(jnp.float32)
    place_row = (lax.rem(lane - tap + half + 2 * rows, rows) == 0).astype(jnp.float32)
    base_col = jnp.dot(
        taps_ref[:, 0, :], place_col, precision=lax.Precision.HIGHEST,
        preferred_element_type=jnp.float32,
    )
    base_row = jnp.dot(
        taps_ref[:, 1, :], place_row, precision=lax.Precision.HIGHEST,
        preferred_element_type=jnp.float32,
    )
    up = lax.broadcasted_iota(jnp.int32, (cols, LANES), 0)
    across = lax.broadcasted_iota(jnp.int32, (cols, LANES), 1)
    near_col = jnp.abs(across - up) <= half
    up_row = lax.broadcasted_iota(jnp.int32, (rows, LANES), 0)
    across_row = lax.rem(lax.broadcasted_iota(jnp.int32, (rows, LANES), 1), rows)
    near_row = jnp.abs(across_row - up_row) <= half
    for c in range(comps):
        wide = jnp.broadcast_to(base_col[c : c + 1, :], (cols, LANES))
        wide = pltpu.roll(wide, 0, 1, stride=1, stride_axis=0)
        high, low = halves(jnp.where(near_col, wide, 0.0))
        cols_ref[c * cols : (c + 1) * cols, :] = jnp.concatenate([high, low], axis=1)
        wide = jnp.broadcast_to(base_row[c : c + 1, :], (rows, LANES))
        wide = pltpu.roll(wide, 0, 1, stride=1, stride_axis=0)
        high, low = halves(jnp.where(near_row, wide, 0.0))
        rows_ref[c * rows : (c + 1) * rows, :] = jnp.concatenate([high, low], axis=1)


def resample_kernel(cfg, first, jobs, with_self, *refs):
    epochs, capacity, per_dev, tiles, count, rows, cols = cfg
    cells = BANDS * per_dev
    n_out = len(jobs) * (epochs - 1) + (1 if with_self else 0)
    places_hbm = refs[:5]
    coeff_hbm, res_hbm, inv_hbm = refs[5:8]
    if first:
        taps_hbm = refs[8]
        rest = refs[9:]
        outs, (cols_ref, rows_ref) = rest[:n_out], rest[n_out : n_out + 2]
        rest = rest[n_out + 2 :]
    else:
        cols_ref, rows_ref = refs[8:10]
        rest = refs[10:]
        outs = rest[:n_out]
        rest = rest[n_out:]
    places = rest[:5]
    owner_ref, slot_ref, band_ref, offset_ref, shift_ref = places
    coeff_ref, res_ref, inv_ref, taps_ref = rest[5:9]
    spread_ref, front_ref, back_ref, block_ref, label_ref, todo_ref, sems = rest[9:]

    pieces = [*zip(places_hbm, places), (coeff_hbm, coeff_ref)]
    if first:
        pieces.append((taps_hbm, taps_ref))
    pieces += [(res_hbm, res_ref), (inv_hbm, inv_ref)]
    fetches = [
        pltpu.make_async_copy(src, dst, sems.at[i]) for i, (src, dst) in enumerate(pieces)
    ]
    for fetch in fetches:
        fetch.start()

    me = lax.axis_index("epoch")
    tile = lax.axis_index("tile")
    for e in range(epochs):
        front_ref[e] = e * capacity
        back_ref[e] = (e + 1) * capacity - 1
    for i in range(epochs * capacity):
        label_ref[i] = 0
        block_ref[i] = 0
    if first:
        fetches[6].wait()
        build_bands(taps_ref, cols_ref, rows_ref)
    for fetch in fetches[:5]:
        fetch.wait()

    def place(b, carry):
        off = offset_ref[b]
        target = tile + off - 1

        @pl.when((target >= 0) & (target < tiles))
        def _():
            o = owner_ref[b]
            front = front_ref[o]
            back = back_ref[o]
            stays = (off == 1).astype(jnp.int32)
            at = jnp.where(off == 1, back, front)
            front_ref[o] = front + 1 - stays
            back_ref[o] = back - stays
            block_ref[at] = b
            label_ref[at] = off * cells + band_ref[b] * per_dev + slot_ref[b] + 1

        return carry

    lax.fori_loop(0, count, place, 0)

    total = jnp.int32(0)
    parts = [(d, start, size) for start, size in jobs for d in range(1, epochs)]
    if with_self:
        parts.append((0, 0, capacity))
    for out_at, (d, start, size) in enumerate(parts):
        o = lax.rem(me + d, epochs)
        for s in range(0, size, 2):
            at = o * capacity + start + s
            todo_ref[0, total] = at
            todo_ref[1, total] = out_at
            todo_ref[2, total] = s
            some = label_ref[at]
            if s + 1 < size:
                some = some + label_ref[at + 1]
            total = total + (some > 0).astype(jnp.int32)

    lane = head_lanes()
    for out_at, (d, start, size) in enumerate(parts):
        if start == 0:
            o = lax.rem(me + d, epochs)
            head = jnp.zeros((HEAD, LANES), jnp.float32)
            for j in range(capacity):
                head = jnp.where(
                    lane == j, label_ref[o * capacity + j].astype(jnp.float32), head
                )
            outs[out_at][size * rows : size * rows + HEAD, :] = head

    fetches[5].wait()
    fetches[-2].wait()
    fetches[-1].wait()
    comps = cols_ref.shape[0] // cols

    def work(i, carry):
        at = todo_ref[0, i]
        out_at = todo_ref[1, i]
        s = todo_ref[2, i]
        blocks = [block_ref[at], block_ref[jnp.minimum(at + 1, epochs * capacity - 1)]]
        sides = []
        for b in blocks:
            high, low = halves(inv_ref[b] * res_ref[b].astype(jnp.float32))
            sides.append(jnp.concatenate([high, low, high, low], axis=0))
        down = jnp.dot(
            rows_ref[...], jnp.concatenate(sides, axis=1), preferred_element_type=jnp.float32
        )
        for c in range(comps):
            for g in range(2):
                part = down[c * rows : (c + 1) * rows, g * cols : (g + 1) * cols]
                high, low = halves(part * coeff_ref[c, blocks[g]])
                spread_ref[g * rows : (g + 1) * rows, c * cols : (c + 1) * cols] = high
                spread_ref[(2 + g) * rows : (3 + g) * rows, c * cols : (c + 1) * cols] = low
        both = jnp.dot(spread_ref[...], cols_ref[...], preferred_element_type=jnp.float32)
        lanes = lax.broadcasted_iota(jnp.int32, (rows, cols), 1)
        for g in range(2):
            high = both[g * rows : (g + 1) * rows]
            low = both[(2 + g) * rows : (3 + g) * rows]
            image = high[:, :cols] + (high[:, cols:] + low[:, :cols])
            shift = shift_ref[blocks[g]]
            image = jnp.where(lanes >= shift, pltpu.roll(image, shift, 1), 0.0)
            for k, (d, start, size) in enumerate(parts):
                last = size % 2 == 1

                @pl.when((out_at == k) & ((s + g < size) if last else True))
                def _():
                    outs[k][pl.ds(pl.multiple_of((s + g) * rows, rows), rows), :] = image

        return carry

    lax.fori_loop(0, total, work, 0)


def read_heads(sources, head_refs, sems):
    copies = [
        pltpu.make_async_copy(src.at[pl.ds(src.shape[0] - HEAD, 1)], dst, sems.at[i])
        for i, (src, dst) in enumerate(zip(sources, head_refs))
    ]
    for copy in copies:
        copy.start()
    for copy in copies:
        copy.wait()


PITCH = 1024


class Queues:
    def __init__(self, cfg, chunks, sends):
        epochs, capacity = cfg[:2]
        self.sources = [(0, 0, 0, capacity)] + [
            (k, d, start, size) for k, (start, size) in enumerate(chunks) for d in range(1, epochs)
        ]
        self.slots = epochs * capacity
        self.waves = len(chunks)
        self.ends = 3 * self.slots + 1
        self.limits = self.ends + 3 * len(self.sources)
        self.size = self.limits + 2 * 2 * self.waves
        self.sends = sends

    def entry(self, which, i):
        return which * self.slots + i

    def end(self, which, source):
        return self.ends + which * len(self.sources) + source

    def limit(self, side, wave):
        return self.limits + 2 * (side * self.waves + wave)

    def fill(self, table, labels, cells):
        counts = (jnp.int32(0),) * 3
        for at, (k, d, start, size) in enumerate(self.sources):

            def step(j, counts, d=d, start=start):
                label = labels(d, start + j)
                kind = (label > cells).astype(jnp.int32) + (label > 2 * cells).astype(jnp.int32)
                some = label > 0
                n = jnp.where(kind == 0, counts[0], jnp.where(kind == 1, counts[1], counts[2]))
                place = jnp.where(some, kind * self.slots + n, 3 * self.slots)
                table[place] = j * PITCH + label - 1 - kind * cells
                return tuple(
                    c + (some & (kind == w)).astype(jnp.int32) for w, c in enumerate(counts)
                )

            counts = lax.fori_loop(0, size, step, counts)
            for w in range(3):
                table[self.end(w, at)] = counts[w]
        for side, which in enumerate((0, 2)):
            sent = jnp.int32(0)
            for k in range(self.waves):
                last = max(i for i, source in enumerate(self.sources) if source[0] == k)
                table[self.limit(side, k)] = sent
                sent = jnp.minimum(table[self.end(which, last)], sent + self.sends[k])
                table[self.limit(side, k) + 1] = sent


def collect_kernel(cfg, queues, k, *refs):
    epochs, _, per_dev, _, _, rows, _ = cfg
    cells = BANDS * per_dev
    known = [i for i, source in enumerate(queues.sources) if source[0] <= k]
    if k == 0:
        sources, rest = refs[: len(known)], refs[len(known) :]
        prev_ref, next_ref, table = rest[:3]
        head_refs, sems = rest[3 : 3 + epochs], rest[3 + epochs]
        read_heads(sources, head_refs, sems)
        queues.fill(table, lambda d, j: head_refs[d][0, j].astype(jnp.int32), cells)
    else:
        table, sources, rest = refs[0], refs[1 : 1 + len(known)], refs[1 + len(known) :]
        prev_ref, next_ref = rest[:2]
    lane = head_lanes()
    cap = queues.sends[k]
    for side, (which, dst) in enumerate(((0, prev_ref), (2, next_ref))):
        first = table[queues.limit(side, k)]
        last = table[queues.limit(side, k) + 1]
        for i, src in zip(known, sources):
            low = table[queues.end(which, i - 1)] if i else 0
            high = table[queues.end(which, i)]

            def step(r, carry, which=which, src=src, dst=dst, first=first):
                j = table[queues.entry(which, r)] // PITCH
                dst[pl.ds(pl.multiple_of((r - first) * rows, rows), rows), :] = src[
                    pl.ds(pl.multiple_of(j * rows, rows), rows), :
                ]
                return carry

            lax.fori_loop(jnp.maximum(low, first), jnp.minimum(high, last), step, 0)

        def mark(r, head, which=which, first=first):
            cell = table[queues.entry(which, r)] % PITCH
            return jnp.where(lane == r - first, cell.astype(jnp.float32), head)

        amount = jnp.where(lane == LANES - 1, (last - first).astype(jnp.float32), 0.0)
        dst[cap * rows : cap * rows + HEAD, :] = lax.fori_loop(first, last, mark, amount)


def add_waves(total_ref, waves, head_refs, rows):
    for src, head in zip(waves, head_refs):

        def step(j, carry, src=src, head=head):
            cell = head[0, j].astype(jnp.int32)
            block = pl.ds(pl.multiple_of(j * rows, rows), rows)
            total_ref[cell] = total_ref[cell] + src[block, :]
            return carry

        lax.fori_loop(0, head[0, LANES - 1].astype(jnp.int32), step, 0)


def settle_kernel(cfg, queues, *refs):
    rows = cfg[5]
    n = len(queues.sources)
    table, sources, rest = refs[0], refs[1 : 1 + n], refs[1 + n :]
    waves = (len(rest) - 2) // 2
    early, total_ref, head_refs, sems = rest[:waves], rest[waves], rest[waves + 1 : -1], rest[-1]
    total_ref[...] = jnp.zeros_like(total_ref)
    for i, src in enumerate(sources):

        def step(r, carry, src=src):
            entry = table[queues.entry(1, r)]
            cell = entry % PITCH
            block = pl.ds(pl.multiple_of((entry // PITCH) * rows, rows), rows)
            total_ref[cell] = total_ref[cell] + src[block, :]
            return carry

        low = table[queues.end(1, i - 1)] if i else 0
        lax.fori_loop(low, table[queues.end(1, i)], step, 0)
    read_heads(early, head_refs, sems)
    add_waves(total_ref, early, head_refs, rows)


def finish_kernel(rows, *refs):
    waves = (len(refs) - 3) // 2
    total_ref, sources, out_ref = refs[0], refs[1 : 1 + waves], refs[1 + waves]
    head_refs, sems = refs[2 + waves : -1], refs[-1]
    out_ref[...] = total_ref[...]
    read_heads(sources, head_refs, sems)
    add_waves(out_ref, sources, head_refs, rows)


def on_device(
    tiles,
    epochs,
    residual,
    inv_variance,
    psf_coeff,
    psf_taps,
    patch_owner,
    patch_slot,
    band_id,
    tile_offset,
    col_shift,
):
    count, rows, cols = residual.shape[1:]
    comps = psf_taps.shape[0]
    capacity = max(2, min(count // 2, 64 // epochs))
    per_dev = PATCHES // epochs
    cells = BANDS * per_dev
    cfg = (epochs, capacity, per_dev, tiles, count, rows, cols)
    chunks = plan_chunks(capacity)
    n = epochs - 1
    f32 = jnp.float32
    smem = pl.BlockSpec(memory_space=SMEM)
    vmem = pl.BlockSpec(memory_space=VMEM)
    hbm = pl.BlockSpec(memory_space=pltpu.HBM)

    def slab(slots):
        return jax.ShapeDtypeStruct((slots * rows + HEAD, cols), f32)

    inputs = (
        patch_owner.reshape(count),
        patch_slot.reshape(count),
        band_id.reshape(count),
        tile_offset.reshape(count),
        col_shift.reshape(count),
        psf_coeff[0].T,
        residual[0],
        inv_variance[0],
        psf_taps,
    )
    inputs = tuple(pltpu.with_memory_space_constraint(x, pltpu.HBM) for x in inputs)
    pairs = epochs * capacity
    scratch = [
        *[SMEM((count,), jnp.int32)] * 5,
        SMEM((comps, count), f32),
        VMEM((count, rows, cols), residual.dtype),
        VMEM((count, rows, cols), f32),
        VMEM(psf_taps.shape, f32),
        VMEM((4 * rows, comps * cols), jnp.bfloat16),
        SMEM((epochs,), jnp.int32),
        SMEM((epochs,), jnp.int32),
        SMEM((epochs * capacity,), jnp.int32),
        SMEM((epochs * capacity,), jnp.int32),
        SMEM((3, pairs + 1), jnp.int32),
        pltpu.SemaphoreType.DMA((9,)),
    ]

    params = pltpu.CompilerParams(vmem_limit_bytes=24 * MIB)
    band_shapes = [
        jax.ShapeDtypeStruct((comps * cols, 2 * cols), jnp.bfloat16),
        jax.ShapeDtypeStruct((comps * rows, 4 * rows), jnp.bfloat16),
    ]
    head_jobs, tail_jobs = chunks[:1], chunks[1:]
    made = pl.pallas_call(
        functools.partial(resample_kernel, cfg, True, head_jobs, False),
        out_shape=[slab(size) for _, size in head_jobs for _ in range(n)] + band_shapes,
        in_specs=[hbm] * 9,
        out_specs=[vmem] * (n + 2),
        scratch_shapes=scratch,
        compiler_params=params,
        name="resample_head",
    )(*inputs)
    slabs = [list(made[:n])]
    bands = made[n:]
    made = pl.pallas_call(
        functools.partial(resample_kernel, cfg, False, tail_jobs, True),
        out_shape=[slab(size) for _, size in tail_jobs for _ in range(n)] + [slab(capacity)],
        in_specs=[hbm] * 8 + [vmem] * 2,
        out_specs=[vmem] * (n * len(tail_jobs) + 1),
        scratch_shapes=scratch,
        compiler_params=params,
        name="resample_tail",
    )(*inputs[:-1], *bands)
    for k in range(len(tail_jobs)):
        slabs.append(list(made[k * n : (k + 1) * n]))
    own = made[-1]

    def turn(x, d):
        return lax.ppermute(x, "epoch", [(i, (i + d) % epochs) for i in range(epochs)])

    def beside(x, d):
        route = [(i, i + d) for i in range(tiles) if 0 <= i + d < tiles]
        return lax.ppermute(x, "tile", route)

    sends = [
        (capacity if k == 0 else 0) + n * size for k, (_, size) in enumerate(chunks)
    ]
    queues = Queues(cfg, chunks, sends)
    sources = [own]
    waves = []
    table = None
    for k in range(len(chunks)):
        sources += [turn(slabs[k][d - 1], d) for d in range(1, epochs)]
        out_shape = [slab(sends[k])] * 2
        out_specs = [vmem] * 2
        extra = []
        if k == 0:
            out_shape.append(jax.ShapeDtypeStruct((queues.size,), jnp.int32))
            out_specs.append(smem)
            extra = [SMEM((1, LANES), f32)] * epochs + [pltpu.SemaphoreType.DMA((epochs,))]
        result = pl.pallas_call(
            functools.partial(collect_kernel, cfg, queues, k),
            out_shape=out_shape,
            in_specs=([smem] if k else []) + [vmem] * len(sources),
            out_specs=out_specs,
            scratch_shapes=extra,
            compiler_params=params,
        )(*([table] if k else []), *sources)
        if k == 0:
            table = result[2]
        waves.append([beside(result[0], -1), beside(result[1], 1)])
    early = [x for wave in waves[:-1] for x in wave]
    late = waves[-1]
    total_shape = jax.ShapeDtypeStruct((cells, rows, cols), f32)

    def heads(arrays):
        return [SMEM((1, LANES), f32)] * len(arrays) + [
            pltpu.SemaphoreType.DMA((len(arrays),))
        ]

    total = pl.pallas_call(
        functools.partial(settle_kernel, cfg, queues),
        out_shape=total_shape,
        in_specs=[smem] + [vmem] * (len(sources) + len(early)),
        out_specs=vmem,
        scratch_shapes=heads(early),
        compiler_params=params,
        name="settle",
    )(table, *sources, *early)
    out = pl.pallas_call(
        functools.partial(finish_kernel, rows),
        out_shape=total_shape,
        in_specs=[vmem] * (1 + len(late)),
        out_specs=vmem,
        scratch_shapes=heads(late),
        compiler_params=params,
        name="finish",
    )(total, *late)
    return out.reshape(1, BANDS, per_dev, rows, cols)


def solution(mesh):
    in_specs = (
        P("tile", "epoch", None, None),
        P("tile", "epoch", None, None),
        P("tile", "epoch", None),
        P(),
        P("tile", "epoch", None),
        P("tile", "epoch"),
        P("tile", "epoch"),
        P("tile", "epoch"),
        P("tile", "epoch"),
    )
    out_specs = P("tile", None, "epoch", None, None)
    epochs = mesh.shape["epoch"]
    device = functools.partial(on_device, mesh.shape["tile"], epochs)

    return jax.shard_map(device, mesh=mesh, in_specs=in_specs, out_specs=out_specs, check_vma=False)
```

profile of v0, /device:TPU:28, one launch (start us, length us, event | category | flops | bytes accessed | tf_op | source)
XLA Modules:
  0.0 97.9 jit_solution(2424667451747651390)
XLA Ops:
  0.0 7.2 %resample_head.1 = (f32[264,128]{1,0:T(8,128)S(1)}, f32[264,128]{1,0:T(8,128)S(1)}, f32[264,128]{1,0:T(8,128)S(1)}, bf16[2048,256]{1,0:T(8,128)(2,1)S(1)}, bf16[1024,256]{1,0:T(8,128)(2,1)S(1)}) custom-call(s32[32]{0:T(128)} %bitcast.17, s32[32]{0:T(128)} %bitcast.19, s32[32]{0:T(128)} %bitcast.21, s32[32]{0:T(128)} %bitcast.23, s32[32]{0:T(128)} %bitcast.25, ...), custom_call_target="tpu_custom_call" | custom-call | tf_op jit(solution)/shard_map/resample_head/pallas_call | solution.py:418
  7.3 0.3 collective-permute-start
  7.5 2.7 %collective-permute-start.1 = (f32[264,128]{1,0:T(8,128)S(1)}, f32[264,128]{1,0:T(8,128)S(1)}, u32[]{:S(2)}, u32[]{:S(2)}) collective-permute-start(f32[264,128]{1,0:T(8,128)S(1)} %get-tuple-element.28), channel_id=1, source_target_pairs={{0,2},{1,3},{2,0},{3,1},{4,6},{5,7},{6,4},{7,5},{8,10},{9,11},{10,... | collective-permute-start | bytes 405512 | tf_op jit(solution)/shard_map/ppermute | solution.py:443
  10.2 0.5 collective-permute-start.2
  10.7 14.6 %resample_tail.1 = (f32[520,128]{1,0:T(8,128)S(1)}, f32[520,128]{1,0:T(8,128)S(1)}, f32[520,128]{1,0:T(8,128)S(1)}, f32[264,128]{1,0:T(8,128)S(1)}, f32[264,128]...) custom-call(s32[32]{0:T(128)} %bitcast.18, s32[32]{0:T(128)} %bitcast.20, s32[32]{0:T(128)} %bitcast.22, ...), custom_call_target="tpu_custom_call" | custom-call | tf_op jit(solution)/shard_map/resample_tail/pallas_call | solution.py:429
  25.3 0.0 collective-permute-done.refs_1_.refs_2_
  25.3 0.0 collective-permute-done.2.refs_3_.refs_4_
  25.3 2.9 %shard_map.91 = (f32[1800,128]{1,0:T(8,128)S(1)}, f32[1800,128]{1,0:T(8,128)S(1)}, s32[235]{0:T(256)S(1)}) custom-call(f32[1032,128]{1,0:T(8,128)S(1)} %get-tuple-element.26.refs_0_.refs_1_, f32[264,128]{1,0:T(8,128)S(1)} %collective-permute-done.refs_1_.refs_2_, f32[264,128]{1,0:T(8,128)S(1)} %collective-permute-done.1.refs_2_.refs_3_, ...), custom_call_target="tpu_custom_call" | custom-call | tf_op jit(solution)/shard_map/pallas_call | solution.py:465
  28.2 1.9 %collective-permute-start.9 = (f32[1800,128]{1,0:T(8,128)S(1)}, f32[1800,128]{1,0:T(8,128)S(1)}, u32[]{:S(2)}, u32[]{:S(2)}) collective-permute-start(f32[1800,128]{1,0:T(8,128)S(1)} %get-tuple-element.37), channel_id=1, source_target_pairs={{4,0},{8,4},{12,8},{16,12},{20,16},{24,20},{28,24},{5,1},{9,5},{13... | collective-permute-start | bytes 2764808 | tf_op jit(solution)/shard_map/ppermute | solution.py:447
  30.1 3.5 %collective-permute-start.3 = (f32[520,128]{1,0:T(8,128)S(1)}, f32[520,128]{1,0:T(8,128)S(1)}, u32[]{:S(2)}, u32[]{:S(2)}) collective-permute-start(f32[520,128]{1,0:T(8,128)S(1)} %get-tuple-element.31), channel_id=1, source_target_pairs={{0,1},{1,2},{2,3},{3,0},{4,5},{5,6},{6,7},{7,4},{8,9},{9,10},{10,1... | collective-permute-start | bytes 798728 | tf_op jit(solution)/shard_map/ppermute | solution.py:443
  33.6 0.0 collective-permute-start.4
  33.6 0.6 collective-permute-start.5
  34.2 1.9 %collective-permute-start.10 = (f32[1800,128]{1,0:T(8,128)S(1)}, f32[1800,128]{1,0:T(8,128)S(1)}, u32[]{:S(2)}, u32[]{:S(2)}) collective-permute-start(f32[1800,128]{1,0:T(8,128)S(1)} %get-tuple-element.38), channel_id=1, source_target_pairs={{0,4},{4,8},{8,12},{12,16},{16,20},{20,24},{24,28},{1,5},{5,9},{9,... | collective-permute-start | bytes 2764808 | tf_op jit(solution)/shard_map/ppermute | solution.py:447
  36.2 5.8 %collective-permute-done.3.refs_5_ = f32[520,128]{1,0:T(8,128)S(1)} collective-permute-done((f32[520,128]{1,0:T(8,128)S(1)}, f32[520,128]{1,0:T(8,128)S(1)}, u32[]{:S(2)}, u32[]{:S(2)}) %collective-permute-start.3) | collective-permute-done | bytes 266272 | tf_op jit(solution)/shard_map/ppermute | solution.py:443
  42.0 2.8 %collective-permute-start.6 = (f32[264,128]{1,0:T(8,128)S(1)}, f32[264,128]{1,0:T(8,128)S(1)}, u32[]{:S(2)}, u32[]{:S(2)}) collective-permute-start(f32[264,128]{1,0:T(8,128)S(1)} %get-tuple-element.34), channel_id=1, source_target_pairs={{0,1},{1,2},{2,3},{3,0},{4,5},{5,6},{6,7},{7,4},{8,9},{9,10},{10,1... | collective-permute-start | bytes 405512 | tf_op jit(solution)/shard_map/ppermute | solution.py:443
  44.8 10.5 %collective-permute-done.4.refs_6_ = f32[520,128]{1,0:T(8,128)S(1)} collective-permute-done((f32[520,128]{1,0:T(8,128)S(1)}, f32[520,128]{1,0:T(8,128)S(1)}, u32[]{:S(2)}, u32[]{:S(2)}) %collective-permute-start.4) | collective-permute-done | bytes 266272 | tf_op jit(solution)/shard_map/ppermute | solution.py:443
  55.3 0.0 collective-permute-done.5.refs_7_
  55.3 0.8 shard_map.92
  56.1 3.0 %collective-permute-start.11 = (f32[1544,128]{1,0:T(8,128)S(1)}, f32[1544,128]{1,0:T(8,128)S(1)}, u32[]{:S(2)}, u32[]{:S(2)}) collective-permute-start(f32[1544,128]{1,0:T(8,128)S(1)} %get-tuple-element.39), channel_id=1, source_target_pairs={{4,0},{8,4},{12,8},{16,12},{20,16},{24,20},{28,24},{5,1},{9,5},{13... | collective-permute-start | bytes 2371592 | tf_op jit(solution)/shard_map/ppermute | solution.py:447
  59.1 1.9 %collective-permute-start.12 = (f32[1544,128]{1,0:T(8,128)S(1)}, f32[1544,128]{1,0:T(8,128)S(1)}, u32[]{:S(2)}, u32[]{:S(2)}) collective-permute-start(f32[1544,128]{1,0:T(8,128)S(1)} %get-tuple-element.40), channel_id=1, source_target_pairs={{0,4},{4,8},{8,12},{12,16},{16,20},{20,24},{24,28},{1,5},{5,9},{9,... | collective-permute-start | bytes 2371592 | tf_op jit(solution)/shard_map/ppermute | solution.py:447
  61.0 0.0 collective-permute-done.6.refs_8_
  61.0 6.8 %collective-permute-start.7 = (f32[264,128]{1,0:T(8,128)S(1)}, f32[264,128]{1,0:T(8,128)S(1)}, u32[]{:S(2)}, u32[]{:S(2)}) collective-permute-start(f32[264,128]{1,0:T(8,128)S(1)} %get-tuple-element.35), channel_id=1, source_target_pairs={{0,2},{1,3},{2,0},{3,1},{4,6},{5,7},{6,4},{7,5},{8,10},{9,11},{10,... | collective-permute-start | bytes 405512 | tf_op jit(solution)/shard_map/ppermute | solution.py:443
  67.8 7.3 %collective-permute-done.7.refs_9_ = f32[264,128]{1,0:T(8,128)S(1)} collective-permute-done((f32[264,128]{1,0:T(8,128)S(1)}, f32[264,128]{1,0:T(8,128)S(1)}, u32[]{:S(2)}, u32[]{:S(2)}) %collective-permute-start.7) | collective-permute-done | bytes 135200 | tf_op jit(solution)/shard_map/ppermute | solution.py:443
  75.1 0.0 collective-permute-start.8
  75.1 7.5 %collective-permute-done.8.refs_10_ = f32[264,128]{1,0:T(8,128)S(1)} collective-permute-done((f32[264,128]{1,0:T(8,128)S(1)}, f32[264,128]{1,0:T(8,128)S(1)}, u32[]{:S(2)}, u32[]{:S(2)}) %collective-permute-start.8) | collective-permute-done | bytes 135200 | tf_op jit(solution)/shard_map/ppermute | solution.py:443
  82.5 0.8 shard_map.93
  83.3 2.0 %collective-permute-start.13 = (f32[776,128]{1,0:T(8,128)S(1)}, f32[776,128]{1,0:T(8,128)S(1)}, u32[]{:S(2)}, u32[]{:S(2)}) collective-permute-start(f32[776,128]{1,0:T(8,128)S(1)} %get-tuple-element.41), channel_id=1, source_target_pairs={{4,0},{8,4},{12,8},{16,12},{20,16},{24,20},{28,24},{5,1},{9,5},{13... | collective-permute-start | bytes 1191944 | tf_op jit(solution)/shard_map/ppermute | solution.py:447
  85.3 2.3 %collective-permute-start.14 = (f32[776,128]{1,0:T(8,128)S(1)}, f32[776,128]{1,0:T(8,128)S(1)}, u32[]{:S(2)}, u32[]{:S(2)}) collective-permute-start(f32[776,128]{1,0:T(8,128)S(1)} %get-tuple-element.42), channel_id=1, source_target_pairs={{0,4},{4,8},{8,12},{12,16},{16,20},{20,24},{24,28},{1,5},{5,9},{9,... | collective-permute-start | bytes 1191944 | tf_op jit(solution)/shard_map/ppermute | solution.py:447
  87.7 1.7 %settle.1.refs_0_ = f32[48,64,128]{2,1,0:T(8,128)S(1)} custom-call(s32[235]{0:T(256)S(1)} %get-tuple-element.30.refs_0_, f32[1032,128]{1,0:T(8,128)S(1)} %get-tuple-element.26.refs_0_.refs_1_, f32[264,128]{1,0:T(8,128)S(1)} %collective-permute-done.refs_1_.refs_2_, f32[264,128]{1,0:T(8,128)S(1)} %collective-permute-done.1.refs_2_.refs_3_, ...), custom_call_target="tpu_custom_call" | custom-call | tf_op jit(solution)/shard_map/settle/pallas_call | solution.py:485
  89.4 3.2 %collective-permute-done.13.refs_1_ = f32[776,128]{1,0:T(8,128)S(1)} collective-permute-done((f32[776,128]{1,0:T(8,128)S(1)}, f32[776,128]{1,0:T(8,128)S(1)}, u32[]{:S(2)}, u32[]{:S(2)}) %collective-permute-start.13) | collective-permute-done | bytes 397344 | tf_op jit(solution)/shard_map/ppermute | solution.py:447
  92.6 3.6 %collective-permute-done.14.refs_2_ = f32[776,128]{1,0:T(8,128)S(1)} collective-permute-done((f32[776,128]{1,0:T(8,128)S(1)}, f32[776,128]{1,0:T(8,128)S(1)}, u32[]{:S(2)}, u32[]{:S(2)}) %collective-permute-start.14) | collective-permute-done | bytes 397344 | tf_op jit(solution)/shard_map/ppermute | solution.py:447
  96.2 1.7 %finish.1 = f32[48,64,128]{2,1,0:T(8,128)} custom-call(f32[48,64,128]{2,1,0:T(8,128)S(1)} %settle.1.refs_0_, f32[776,128]{1,0:T(8,128)S(1)} %collective-permute-done.13.refs_1_, f32[776,128]{1,0:T(8,128)S(1)} %collective-permute-done.14.refs_2_), custom_call_target="tpu_custom_call" | custom-call | tf_op jit(solution)/shard_map/finish/pallas_call | solution.py:494
  (5 shorter events, 0.0 us)
Async XLA Ops:
  7.3 18.0 %collective-permute-start = (f32[264,128]{1,0:T(8,128)S(1)}, f32[264,128]{1,0:T(8,128)S(1)}, u32[]{:S(2)}, u32[]{:S(2)}) collective-permute-start(f32[264,128]{1,0:T(8,128)S(1)} %get-tuple-element.27), channel_id=1, source_target_pairs={{0,1},{1,2},{2,3},{3,0},{4,5},{5,6},{6,7},{7,4},{8,9},{9,10},{10,1... | collective-permute-start | bytes 405512 | tf_op jit(solution)/shard_map/ppermute | solution.py:443
  7.5 17.7 %collective-permute-start.1 = (f32[264,128]{1,0:T(8,128)S(1)}, f32[264,128]{1,0:T(8,128)S(1)}, u32[]{:S(2)}, u32[]{:S(2)}) collective-permute-start(f32[264,128]{1,0:T(8,128)S(1)} %get-tuple-element.28), channel_id=1, source_target_pairs={{0,2},{1,3},{2,0},{3,1},{4,6},{5,7},{6,4},{7,5},{8,10},{9,11},{10,... | collective-permute-start | bytes 405512 | tf_op jit(solution)/shard_map/ppermute | solution.py:443
  10.2 15.1 %collective-permute-start.2 = (f32[264,128]{1,0:T(8,128)S(1)}, f32[264,128]{1,0:T(8,128)S(1)}, u32[]{:S(2)}, u32[]{:S(2)}) collective-permute-start(f32[264,128]{1,0:T(8,128)S(1)} %get-tuple-element.29), channel_id=1, source_target_pairs={{0,3},{1,0},{2,1},{3,2},{4,7},{5,4},{6,5},{7,6},{8,11},{9,8},{10,9... | collective-permute-start | bytes 405512 | tf_op jit(solution)/shard_map/ppermute | solution.py:443
  28.2 57.1 %collective-permute-start.9 = (f32[1800,128]{1,0:T(8,128)S(1)}, f32[1800,128]{1,0:T(8,128)S(1)}, u32[]{:S(2)}, u32[]{:S(2)}) collective-permute-start(f32[1800,128]{1,0:T(8,128)S(1)} %get-tuple-element.37), channel_id=1, source_target_pairs={{4,0},{8,4},{12,8},{16,12},{20,16},{24,20},{28,24},{5,1},{9,5},{13... | collective-permute-start | bytes 2764808 | tf_op jit(solution)/shard_map/ppermute | solution.py:447
  30.1 11.9 %collective-permute-start.3 = (f32[520,128]{1,0:T(8,128)S(1)}, f32[520,128]{1,0:T(8,128)S(1)}, u32[]{:S(2)}, u32[]{:S(2)}) collective-permute-start(f32[520,128]{1,0:T(8,128)S(1)} %get-tuple-element.31), channel_id=1, source_target_pairs={{0,1},{1,2},{2,3},{3,0},{4,5},{5,6},{6,7},{7,4},{8,9},{9,10},{10,1... | collective-permute-start | bytes 798728 | tf_op jit(solution)/shard_map/ppermute | solution.py:443
  33.6 21.7 %collective-permute-start.4 = (f32[520,128]{1,0:T(8,128)S(1)}, f32[520,128]{1,0:T(8,128)S(1)}, u32[]{:S(2)}, u32[]{:S(2)}) collective-permute-start(f32[520,128]{1,0:T(8,128)S(1)} %get-tuple-element.32), channel_id=1, source_target_pairs={{0,2},{1,3},{2,0},{3,1},{4,6},{5,7},{6,4},{7,5},{8,10},{9,11},{10,... | collective-permute-start | bytes 798728 | tf_op jit(solution)/shard_map/ppermute | solution.py:443
  33.6 21.7 %collective-permute-start.5 = (f32[520,128]{1,0:T(8,128)S(1)}, f32[520,128]{1,0:T(8,128)S(1)}, u32[]{:S(2)}, u32[]{:S(2)}) collective-permute-start(f32[520,128]{1,0:T(8,128)S(1)} %get-tuple-element.33), channel_id=1, source_target_pairs={{0,3},{1,0},{2,1},{3,2},{4,7},{5,4},{6,5},{7,6},{8,11},{9,8},{10,9... | collective-permute-start | bytes 798728 | tf_op jit(solution)/shard_map/ppermute | solution.py:443
  34.2 53.4 %collective-permute-start.10 = (f32[1800,128]{1,0:T(8,128)S(1)}, f32[1800,128]{1,0:T(8,128)S(1)}, u32[]{:S(2)}, u32[]{:S(2)}) collective-permute-start(f32[1800,128]{1,0:T(8,128)S(1)} %get-tuple-element.38), channel_id=1, source_target_pairs={{0,4},{4,8},{8,12},{12,16},{16,20},{20,24},{24,28},{1,5},{5,9},{9,... | collective-permute-start | bytes 2764808 | tf_op jit(solution)/shard_map/ppermute | solution.py:447
  42.0 19.0 %collective-permute-start.6 = (f32[264,128]{1,0:T(8,128)S(1)}, f32[264,128]{1,0:T(8,128)S(1)}, u32[]{:S(2)}, u32[]{:S(2)}) collective-permute-start(f32[264,128]{1,0:T(8,128)S(1)} %get-tuple-element.34), channel_id=1, source_target_pairs={{0,1},{1,2},{2,3},{3,0},{4,5},{5,6},{6,7},{7,4},{8,9},{9,10},{10,1... | collective-permute-start | bytes 405512 | tf_op jit(solution)/shard_map/ppermute | solution.py:443
  56.1 31.6 %collective-permute-start.11 = (f32[1544,128]{1,0:T(8,128)S(1)}, f32[1544,128]{1,0:T(8,128)S(1)}, u32[]{:S(2)}, u32[]{:S(2)}) collective-permute-start(f32[1544,128]{1,0:T(8,128)S(1)} %get-tuple-element.39), channel_id=1, source_target_pairs={{4,0},{8,4},{12,8},{16,12},{20,16},{24,20},{28,24},{5,1},{9,5},{13... | collective-permute-start | bytes 2371592 | tf_op jit(solution)/shard_map/ppermute | solution.py:447
  59.1 28.6 %collective-permute-start.12 = (f32[1544,128]{1,0:T(8,128)S(1)}, f32[1544,128]{1,0:T(8,128)S(1)}, u32[]{:S(2)}, u32[]{:S(2)}) collective-permute-start(f32[1544,128]{1,0:T(8,128)S(1)} %get-tuple-element.40), channel_id=1, source_target_pairs={{0,4},{4,8},{8,12},{12,16},{16,20},{20,24},{24,28},{1,5},{5,9},{9,... | collective-permute-start | bytes 2371592 | tf_op jit(solution)/shard_map/ppermute | solution.py:447
  61.0 14.0 %collective-permute-start.7 = (f32[264,128]{1,0:T(8,128)S(1)}, f32[264,128]{1,0:T(8,128)S(1)}, u32[]{:S(2)}, u32[]{:S(2)}) collective-permute-start(f32[264,128]{1,0:T(8,128)S(1)} %get-tuple-element.35), channel_id=1, source_target_pairs={{0,2},{1,3},{2,0},{3,1},{4,6},{5,7},{6,4},{7,5},{8,10},{9,11},{10,... | collective-permute-start | bytes 405512 | tf_op jit(solution)/shard_map/ppermute | solution.py:443
  75.1 7.5 %collective-permute-start.8 = (f32[264,128]{1,0:T(8,128)S(1)}, f32[264,128]{1,0:T(8,128)S(1)}, u32[]{:S(2)}, u32[]{:S(2)}) collective-permute-start(f32[264,128]{1,0:T(8,128)S(1)} %get-tuple-element.36), channel_id=1, source_target_pairs={{0,3},{1,0},{2,1},{3,2},{4,7},{5,4},{6,5},{7,6},{8,11},{9,8},{10,9... | collective-permute-start | bytes 405512 | tf_op jit(solution)/shard_map/ppermute | solution.py:443
  83.3 9.4 %collective-permute-start.13 = (f32[776,128]{1,0:T(8,128)S(1)}, f32[776,128]{1,0:T(8,128)S(1)}, u32[]{:S(2)}, u32[]{:S(2)}) collective-permute-start(f32[776,128]{1,0:T(8,128)S(1)} %get-tuple-element.41), channel_id=1, source_target_pairs={{4,0},{8,4},{12,8},{16,12},{20,16},{24,20},{28,24},{5,1},{9,5},{13... | collective-permute-start | bytes 1191944 | tf_op jit(solution)/shard_map/ppermute | solution.py:447
  85.3 10.9 %collective-permute-start.14 = (f32[776,128]{1,0:T(8,128)S(1)}, f32[776,128]{1,0:T(8,128)S(1)}, u32[]{:S(2)}, u32[]{:S(2)}) collective-permute-start(f32[776,128]{1,0:T(8,128)S(1)} %get-tuple-element.42), channel_id=1, source_target_pairs={{0,4},{4,8},{8,12},{12,16},{16,20},{20,24},{24,28},{1,5},{5,9},{9,... | collective-permute-start | bytes 1191944 | tf_op jit(solution)/shard_map/ppermute | solution.py:447
where the time goes:
time: 98.2 us; the launch traced here: 97.9 us
  waiting for transfers between devices  37.8 us (38%)
  starting transfers between devices  30.2 us (31%)
  Pallas kernels  29.7 us (30%)
    ppermute x9, waiting for transfers between devices, turn(): lax.ppermute(x, 'epoch', [(i, (i + d) % epochs) for i in range(epochs)])  31 us
    ppermute x9, starting transfers between devices, turn(): lax.ppermute(x, 'epoch', [(i, (i + d) % epochs) for i in range(epochs)])  17.2 us
    pallas_call x1, Pallas kernels, on_device(): pl.pallas_call(functools.partial(resample_kernel, cfg, False, tail_jobs,...  14.6 us
    ppermute x6, starting transfers between devices, beside(): return lax.ppermute(x, 'tile', route)  13.1 us
    pallas_call x1, Pallas kernels, on_device(): pl.pallas_call(functools.partial(resample_kernel, cfg, True, head_jobs, F...  7.24 us
    ppermute x6, waiting for transfers between devices, beside(): return lax.ppermute(x, 'tile', route)  6.79 us
    pallas_call x3, Pallas kernels, on_device(): pl.pallas_call(functools.partial(collect_kernel, cfg, queues, k), out_sha...  4.42 us
  transfers between devices with their start and end apart: 15, of which 6 were waited for; matrix products, arithmetic and copies ran while one was open for 0% of the time, Pallas kernels for 18%

commit v1 on v0

--- a/solution.py
+++ b/solution.py
@@ -72,50 +72,14 @@
         rows_ref[c * rows : (c + 1) * rows, :] = jnp.concatenate([high, low], axis=1)
 
 
-def resample_kernel(cfg, first, jobs, with_self, *refs):
-    epochs, capacity, per_dev, tiles, count, rows, cols = cfg
+def fill_slots(cfg, places, block_ref, label_ref, front_ref, back_ref):
+    epochs, capacity, per_dev, tiles, count, _, _ = cfg
     cells = BANDS * per_dev
-    n_out = len(jobs) * (epochs - 1) + (1 if with_self else 0)
-    places_hbm = refs[:5]
-    coeff_hbm, res_hbm, inv_hbm = refs[5:8]
-    if first:
-        taps_hbm = refs[8]
-        rest = refs[9:]
-        outs, (cols_ref, rows_ref) = rest[:n_out], rest[n_out : n_out + 2]
-        rest = rest[n_out + 2 :]
-    else:
-        cols_ref, rows_ref = refs[8:10]
-        rest = refs[10:]
-        outs = rest[:n_out]
-        rest = rest[n_out:]
-    places = rest[:5]
-    owner_ref, slot_ref, band_ref, offset_ref, shift_ref = places
-    coeff_ref, res_ref, inv_ref, taps_ref = rest[5:9]
-    spread_ref, front_ref, back_ref, block_ref, label_ref, todo_ref, sems = rest[9:]
-
-    pieces = [*zip(places_hbm, places), (coeff_hbm, coeff_ref)]
-    if first:
-        pieces.append((taps_hbm, taps_ref))
-    pieces += [(res_hbm, res_ref), (inv_hbm, inv_ref)]
-    fetches = [
-        pltpu.make_async_copy(src, dst, sems.at[i]) for i, (src, dst) in enumerate(pieces)
-    ]
-    for fetch in fetches:
-        fetch.start()
-
-    me = lax.axis_index("epoch")
+    owner_ref, slot_ref, band_ref, offset_ref = places
     tile = lax.axis_index("tile")
     for e in range(epochs):
         front_ref[e] = e * capacity
         back_ref[e] = (e + 1) * capacity - 1
-    for i in range(epochs * capacity):
-        label_ref[i] = 0
-        block_ref[i] = 0
-    if first:
-        fetches[6].wait()
-        build_bands(taps_ref, cols_ref, rows_ref)
-    for fetch in fetches[:5]:
-        fetch.wait()
 
     def place(b, carry):
         off = offset_ref[b]
@@ -137,74 +101,126 @@
 
     lax.fori_loop(0, count, place, 0)
 
+
+def resample_kernel(cfg, first, jobs, with_self, *refs):
+    epochs, capacity, _, _, _, rows, cols = cfg
+    slots = epochs * capacity
+    n_out = len(jobs) * (epochs - 1) + (1 if with_self else 0)
+    if first:
+        small_hbm, large_hbm, rest = refs[:6], refs[6:9], refs[9:]
+        outs, rest = rest[:n_out], rest[n_out:]
+        cols_ref, rows_ref, res_ref, inv_ref, block_ref, label_ref = rest[:6]
+        shift_ref, coeff_ref, *places, taps_ref, front_ref, back_ref = rest[6:15]
+        small = [*places, shift_ref, coeff_ref]
+        rest = rest[15:]
+        pieces = [
+            *zip(small_hbm, small),
+            *zip(large_hbm, (taps_ref, res_ref, inv_ref)),
+        ]
+    else:
+        block_ref, label_ref, shift_ref, coeff_ref = refs[:4]
+        cols_ref, rows_ref, res_ref, inv_ref = refs[4:8]
+        outs, rest = refs[8 : 8 + n_out], refs[8 + n_out :]
+        pieces = []
+    spread_refs, todo_ref, sems = rest[:2], rest[2], rest[3]
+    fetches = [
+        pltpu.make_async_copy(src, dst, sems.at[i]) for i, (src, dst) in enumerate(pieces)
+    ]
+    for fetch in fetches:
+        fetch.start()
+
+    if first:
+        for i in range(slots):
+            label_ref[i] = 0
+            block_ref[i] = 0
+        fetches[6].wait()
+        build_bands(taps_ref, cols_ref, rows_ref)
+        for fetch in fetches[:4]:
+            fetch.wait()
+        fill_slots(cfg, places, block_ref, label_ref, front_ref, back_ref)
+
+    me = lax.axis_index("epoch")
     total = jnp.int32(0)
     parts = [(d, start, size) for start, size in jobs for d in range(1, epochs)]
     if with_self:
         parts.append((0, 0, capacity))
-    for out_at, (d, start, size) in enumerate(parts):
+    for k, (d, start, size) in enumerate(parts):
         o = lax.rem(me + d, epochs)
-        for s in range(0, size, 2):
+        for s in range(size):
             at = o * capacity + start + s
-            todo_ref[0, total] = at
-            todo_ref[1, total] = out_at
-            todo_ref[2, total] = s
-            some = label_ref[at]
-            if s + 1 < size:
-                some = some + label_ref[at + 1]
-            total = total + (some > 0).astype(jnp.int32)
+            todo_ref[0, total] = block_ref[at]
+            todo_ref[1, total] = k * slots + s
+            total = total + (label_ref[at] > 0).astype(jnp.int32)
+    for i in range(3):
+        todo_ref[0, total + i] = 0
+        todo_ref[1, total + i] = len(parts) * slots
 
     lane = head_lanes()
-    for out_at, (d, start, size) in enumerate(parts):
-        if start == 0:
-            o = lax.rem(me + d, epochs)
-            head = jnp.zeros((HEAD, LANES), jnp.float32)
-            for j in range(capacity):
-                head = jnp.where(
-                    lane == j, label_ref[o * capacity + j].astype(jnp.float32), head
-                )
-            outs[out_at][size * rows : size * rows + HEAD, :] = head
-
-    fetches[5].wait()
-    fetches[-2].wait()
-    fetches[-1].wait()
+    if any(start == 0 for _, start, _ in parts):
+        head = jnp.zeros((HEAD, LANES), jnp.float32)
+        for j in range(slots):
+            head = jnp.where(lane == j, label_ref[j].astype(jnp.float32), head)
+        for k, (d, start, size) in enumerate(parts):
+            if start == 0:
+                outs[k][size * rows : size * rows + HEAD, :] = head
+
+    for fetch in fetches[4:6] + fetches[7:]:
+        fetch.wait()
     comps = cols_ref.shape[0] // cols
-
-    def work(i, carry):
-        at = todo_ref[0, i]
-        out_at = todo_ref[1, i]
-        s = todo_ref[2, i]
-        blocks = [block_ref[at], block_ref[jnp.minimum(at + 1, epochs * capacity - 1)]]
-        sides = []
-        for b in blocks:
-            high, low = halves(inv_ref[b] * res_ref[b].astype(jnp.float32))
-            sides.append(jnp.concatenate([high, low, high, low], axis=0))
-        down = jnp.dot(
-            rows_ref[...], jnp.concatenate(sides, axis=1), preferred_element_type=jnp.float32
-        )
-        for c in range(comps):
+    lanes = lax.broadcasted_iota(jnp.int32, (rows, cols), 1)
+
+    def work(base, twos):
+        jobs_here = [(todo_ref[0, base + g], todo_ref[1, base + g]) for g in range(2 * twos)]
+        for t in range(twos):
+            blocks = [b for b, _ in jobs_here[2 * t : 2 * t + 2]]
+            spread_ref = spread_refs[t]
+            sides = []
+            for b in blocks:
+                high, low = halves(inv_ref[b] * res_ref[b].astype(jnp.float32))
+                sides.append(jnp.concatenate([high, low, high, low], axis=0))
+            down = jnp.dot(
+                rows_ref[...],
+                jnp.concatenate(sides, axis=1),
+                preferred_element_type=jnp.float32,
+            )
+            for c in range(comps):
+                for g in range(2):
+                    part = down[c * rows : (c + 1) * rows, g * cols : (g + 1) * cols]
+                    high, low = halves(part * coeff_ref[c, blocks[g]])
+                    at = slice(c * cols, (c + 1) * cols)
+                    spread_ref[g * rows : (g + 1) * rows, at] = high
+                    spread_ref[(2 + g) * rows : (3 + g) * rows, at] = low
+        images = []
+        for t in range(twos):
+            both = jnp.dot(
+                spread_refs[t][...], cols_ref[...], preferred_element_type=jnp.float32
+            )
             for g in range(2):
-                part = down[c * rows : (c + 1) * rows, g * cols : (g + 1) * cols]
-                high, low = halves(part * coeff_ref[c, blocks[g]])
-                spread_ref[g * rows : (g + 1) * rows, c * cols : (c + 1) * cols] = high
-                spread_ref[(2 + g) * rows : (3 + g) * rows, c * cols : (c + 1) * cols] = low
-        both = jnp.dot(spread_ref[...], cols_ref[...], preferred_element_type=jnp.float32)
-        lanes = lax.broadcasted_iota(jnp.int32, (rows, cols), 1)
-        for g in range(2):
-            high = both[g * rows : (g + 1) * rows]
-            low = both[(2 + g) * rows : (3 + g) * rows]
-            image = high[:, :cols] + (high[:, cols:] + low[:, :cols])
-            shift = shift_ref[blocks[g]]
-            image = jnp.where(lanes >= shift, pltpu.roll(image, shift, 1), 0.0)
-            for k, (d, start, size) in enumerate(parts):
-                last = size % 2 == 1
-
-                @pl.when((out_at == k) & ((s + g < size) if last else True))
+                b, where = jobs_here[2 * t + g]
+                high = both[g * rows : (g + 1) * rows]
+                low = both[(2 + g) * rows : (3 + g) * rows]
+                image = high[:, :cols] + (high[:, cols:] + low[:, :cols])
+                shift = shift_ref[b]
+                images.append(jnp.where(lanes >= shift, pltpu.roll(image, shift, 1), 0.0))
+        for (_, where), image in zip(jobs_here, images):
+            for k in range(len(parts)):
+
+                @pl.when((where >= k * slots) & (where < (k + 1) * slots))
                 def _():
-                    outs[k][pl.ds(pl.multiple_of((s + g) * rows, rows), rows), :] = image
-
+                    s = pl.multiple_of((where - k * slots) * rows, rows)
+                    outs[k][pl.ds(s, rows), :] = image
+
+    quads = (total + 1) // 4
+
+    def quad(i, carry):
+        work(4 * i, 2)
         return carry
 
-    lax.fori_loop(0, total, work, 0)
+    lax.fori_loop(0, quads, quad, 0)
+
+    @pl.when(total > 4 * quads)
+    def _():
+        work(4 * quads, 1)
 
 
 def read_heads(sources, head_refs, sems):
@@ -233,6 +249,7 @@
         self.limits = self.ends + 3 * len(self.sources)
         self.size = self.limits + 2 * 2 * self.waves
         self.sends = sends
+        self.capacity = capacity
 
     def entry(self, which, i):
         return which * self.slots + i
@@ -270,19 +287,47 @@
                 table[self.limit(side, k) + 1] = sent
 
 
-def collect_kernel(cfg, queues, k, *refs):
-    epochs, _, per_dev, _, _, rows, _ = cfg
+    def overflow(self, heads, cells, ends):
+        slot = lax.broadcasted_iota(jnp.int32, (LANES, LANES), 0)
+        epoch = lax.broadcasted_iota(jnp.int32, (LANES, LANES), 1)
+        mine = lax.div(slot, self.capacity) == epoch
+        over = jnp.zeros((HEAD, LANES), jnp.float32)
+        for low, high in ((0, cells), (2 * cells, 3 * cells)):
+            amount = jnp.zeros((HEAD, LANES), jnp.float32)
+            for head in heads:
+                amount = amount + jnp.where((head > low) & (head <= high), 1.0, 0.0)
+            sent = jnp.zeros((HEAD, LANES), jnp.float32)
+            for end, cap in zip(ends, self.sends):
+                here = jnp.where(mine & (lax.rem(slot, self.capacity) < end), 1.0, 0.0)
+                have = jnp.dot(
+                    amount.astype(jnp.bfloat16),
+                    here.astype(jnp.bfloat16),
+                    preferred_element_type=jnp.float32,
+                )
+                sent = jnp.minimum(have, sent + cap)
+            over = jnp.maximum(over, jnp.where(have > sent, 1.0, 0.0))
+        return over
+
+
+def collect_kernel(cfg, queues, k, ends, *refs):
+    epochs, capacity, per_dev, _, _, rows, _ = cfg
     cells = BANDS * per_dev
     known = [i for i, source in enumerate(queues.sources) if source[0] <= k]
     if k == 0:
         sources, rest = refs[: len(known)], refs[len(known) :]
-        prev_ref, next_ref, table = rest[:3]
-        head_refs, sems = rest[3 : 3 + epochs], rest[3 + epochs]
+        prev_ref, next_ref, table, over_ref = rest[:4]
+        head_refs, sems = rest[4 : 4 + epochs], rest[4 + epochs]
         read_heads(sources, head_refs, sems)
-        queues.fill(table, lambda d, j: head_refs[d][0, j].astype(jnp.int32), cells)
+        mine = lax.axis_index("epoch") * capacity
+        queues.fill(table, lambda d, j: head_refs[d][0, mine + j].astype(jnp.int32), cells)
+        heads = [src[src.shape[0] - HEAD :, :] for src in sources]
+        over = jnp.max(queues.overflow(heads, cells, ends), axis=1, keepdims=True)
+        over_ref[...] = jnp.broadcast_to(over, over_ref.shape)
     else:
-        table, sources, rest = refs[0], refs[1 : 1 + len(known)], refs[1 + len(known) :]
-        prev_ref, next_ref = rest[:2]
+        table, mine_ref, theirs_ref = refs[:3]
+        sources, rest = refs[3 : 3 + len(known)], refs[3 + len(known) :]
+        prev_ref, next_ref, over_ref = rest
+        over_ref[...] = jnp.maximum(mine_ref[...], theirs_ref[...])
     lane = head_lanes()
     cap = queues.sends[k]
     for side, (which, dst) in enumerate(((0, prev_ref), (2, next_ref))):
@@ -344,35 +389,33 @@
 
 
 def finish_kernel(rows, *refs):
-    waves = (len(refs) - 3) // 2
-    total_ref, sources, out_ref = refs[0], refs[1 : 1 + waves], refs[1 + waves]
-    head_refs, sems = refs[2 + waves : -1], refs[-1]
+    total_ref, mine_ref, theirs_ref = refs[:3]
+    waves = (len(refs) - 8) // 2
+    sources, (out_ref, failed_ref) = refs[3 : 3 + waves], refs[3 + waves : 5 + waves]
+    head_refs, (over_ref, said_ref, sems) = refs[5 + waves : -3], refs[-3:]
+    over_ref[...] = jnp.maximum(mine_ref[...], theirs_ref[...])
+    say = pltpu.make_async_copy(over_ref.at[pl.ds(0, 1)], said_ref, sems.at[waves])
+    say.start()
     out_ref[...] = total_ref[...]
     read_heads(sources, head_refs, sems)
     add_waves(out_ref, sources, head_refs, rows)
-
-
-def on_device(
-    tiles,
-    epochs,
-    residual,
-    inv_variance,
-    psf_coeff,
-    psf_taps,
-    patch_owner,
-    patch_slot,
-    band_id,
-    tile_offset,
-    col_shift,
-):
-    count, rows, cols = residual.shape[1:]
+    say.wait()
+    failed_ref[0] = (said_ref[0, 0] > 0.0).astype(jnp.int32)
+
+
+def run(cfg, sends, args):
+    (
+        residual, inv_variance, psf_coeff, psf_taps, patch_owner,
+        patch_slot, band_id, tile_offset, col_shift,
+    ) = args
+    epochs, capacity, per_dev, tiles, count, rows, cols = cfg
     comps = psf_taps.shape[0]
-    capacity = max(2, min(count // 2, 64 // epochs))
-    per_dev = PATCHES // epochs
     cells = BANDS * per_dev
-    cfg = (epochs, capacity, per_dev, tiles, count, rows, cols)
     chunks = plan_chunks(capacity)
+    ends = [start + size for start, size in chunks]
     n = epochs - 1
+    full = [(capacity if k == 0 else 0) + n * size for k, (_, size) in enumerate(chunks)]
+    checked = any(cap < most for cap, most in zip(sends, full))
     f32 = jnp.float32
     smem = pl.BlockSpec(memory_space=SMEM)
     vmem = pl.BlockSpec(memory_space=VMEM)
@@ -388,55 +431,51 @@
         tile_offset.reshape(count),
         col_shift.reshape(count),
         psf_coeff[0].T,
+        psf_taps,
         residual[0],
         inv_variance[0],
-        psf_taps,
     )
     inputs = tuple(pltpu.with_memory_space_constraint(x, pltpu.HBM) for x in inputs)
-    pairs = epochs * capacity
-    scratch = [
-        *[SMEM((count,), jnp.int32)] * 5,
-        SMEM((comps, count), f32),
-        VMEM((count, rows, cols), residual.dtype),
-        VMEM((count, rows, cols), f32),
-        VMEM(psf_taps.shape, f32),
-        VMEM((4 * rows, comps * cols), jnp.bfloat16),
-        SMEM((epochs,), jnp.int32),
-        SMEM((epochs,), jnp.int32),
-        SMEM((epochs * capacity,), jnp.int32),
-        SMEM((epochs * capacity,), jnp.int32),
-        SMEM((3, pairs + 1), jnp.int32),
+    slots = epochs * capacity
+    common = [
+        *[VMEM((4 * rows, comps * cols), jnp.bfloat16)] * 2,
+        SMEM((2, slots + 3), jnp.int32),
         pltpu.SemaphoreType.DMA((9,)),
     ]
-
     params = pltpu.CompilerParams(vmem_limit_bytes=24 * MIB)
-    band_shapes = [
+    kept = [
         jax.ShapeDtypeStruct((comps * cols, 2 * cols), jnp.bfloat16),
         jax.ShapeDtypeStruct((comps * rows, 4 * rows), jnp.bfloat16),
+        jax.ShapeDtypeStruct((count, rows, cols), residual.dtype),
+        jax.ShapeDtypeStruct((count, rows, cols), f32),
     ]
-    head_jobs, tail_jobs = chunks[:1], chunks[1:]
+    kept += [jax.ShapeDtypeStruct((slots,), jnp.int32)] * 2
+    kept += [jax.ShapeDtypeStruct((count,), jnp.int32)]
+    kept += [jax.ShapeDtypeStruct((comps, count), f32)]
     made = pl.pallas_call(
-        functools.partial(resample_kernel, cfg, True, head_jobs, False),
-        out_shape=[slab(size) for _, size in head_jobs for _ in range(n)] + band_shapes,
+        functools.partial(resample_kernel, cfg, True, chunks[:1], False),
+        out_shape=[slab(chunks[0][1]) for _ in range(n)] + kept,
         in_specs=[hbm] * 9,
-        out_specs=[vmem] * (n + 2),
-        scratch_shapes=scratch,
+        out_specs=[vmem] * (n + 4) + [smem] * 4,
+        scratch_shapes=[SMEM((count,), jnp.int32)] * 4
+        + [VMEM(psf_taps.shape, f32)]
+        + [SMEM((epochs,), jnp.int32)] * 2
+        + common,
         compiler_params=params,
-        name="resample_head",
+        name="resample_0",
     )(*inputs)
-    slabs = [list(made[:n])]
-    bands = made[n:]
-    made = pl.pallas_call(
-        functools.partial(resample_kernel, cfg, False, tail_jobs, True),
-        out_shape=[slab(size) for _, size in tail_jobs for _ in range(n)] + [slab(capacity)],
-        in_specs=[hbm] * 8 + [vmem] * 2,
-        out_specs=[vmem] * (n * len(tail_jobs) + 1),
-        scratch_shapes=scratch,
-        compiler_params=params,
-        name="resample_tail",
-    )(*inputs[:-1], *bands)
-    for k in range(len(tail_jobs)):
-        slabs.append(list(made[k * n : (k + 1) * n]))
+    slabs, kept = [list(made[:n])], made[n:]
+    for k in range(1, len(chunks)):
+        last = k == len(chunks) - 1
+        made = pl.pallas_call(
+            functools.partial(resample_kernel, cfg, False, chunks[k : k + 1], last),
+            out_shape=[slab(chunks[k][1]) for _ in range(n)] + [slab(capacity)] * last,
+            in_specs=[smem] * 4 + [vmem] * 4,
+            out_specs=[vmem] * (n + last),
+            scratch_shapes=common,
+            compiler_params=params,
+        )(*kept[4:], *kept[:4])
+        slabs.append(list(made[:n]))
     own = made[-1]
 
     def turn(x, d):
@@ -446,13 +485,15 @@
         route = [(i, i + d) for i in range(tiles) if 0 <= i + d < tiles]
         return lax.ppermute(x, "tile", route)
 
-    sends = [
-        (capacity if k == 0 else 0) + n * size for k, (_, size) in enumerate(chunks)
-    ]
+    def swap(x, k):
+        if not checked:
+            return x
+        return lax.ppermute(x, "tile", [(i, i ^ (1 << k)) for i in range(tiles)])
+
     queues = Queues(cfg, chunks, sends)
     sources = [own]
     waves = []
-    table = None
+    table = over = None
     for k in range(len(chunks)):
         sources += [turn(slabs[k][d - 1], d) for d in range(1, epochs)]
         out_shape = [slab(sends[k])] * 2
@@ -462,16 +503,20 @@
             out_shape.append(jax.ShapeDtypeStruct((queues.size,), jnp.int32))
             out_specs.append(smem)
             extra = [SMEM((1, LANES), f32)] * epochs + [pltpu.SemaphoreType.DMA((epochs,))]
+        out_shape.append(jax.ShapeDtypeStruct((HEAD, LANES), f32))
+        out_specs.append(vmem)
+        told = [over, swap(over, k - 1)] if k else []
         result = pl.pallas_call(
-            functools.partial(collect_kernel, cfg, queues, k),
+            functools.partial(collect_kernel, cfg, queues, k, ends),
             out_shape=out_shape,
-            in_specs=([smem] if k else []) + [vmem] * len(sources),
+            in_specs=([smem] if k else []) + [vmem] * (len(told) + len(sources)),
             out_specs=out_specs,
             scratch_shapes=extra,
             compiler_params=params,
-        )(*([table] if k else []), *sources)
+        )(*([table] if k else []), *told, *sources)
         if k == 0:
             table = result[2]
+        over = result[-1]
         waves.append([beside(result[0], -1), beside(result[1], 1)])
     early = [x for wave in waves[:-1] for x in wave]
     late = waves[-1]
@@ -491,15 +536,43 @@
         compiler_params=params,
         name="settle",
     )(table, *sources, *early)
-    out = pl.pallas_call(
+    out, failed = pl.pallas_call(
         functools.partial(finish_kernel, rows),
-        out_shape=total_shape,
-        in_specs=[vmem] * (1 + len(late)),
-        out_specs=vmem,
-        scratch_shapes=heads(late),
+        out_shape=[total_shape, jax.ShapeDtypeStruct((1,), jnp.int32)],
+        in_specs=[vmem] * (3 + len(late)),
+        out_specs=[vmem, smem],
+        scratch_shapes=[
+            *[SMEM((1, LANES), f32)] * len(late),
+            VMEM((HEAD, LANES), f32),
+            SMEM((1, LANES), f32),
+            pltpu.SemaphoreType.DMA((len(late) + 1,)),
+        ],
         compiler_params=params,
         name="finish",
-    )(total, *late)
+    )(total, over, swap(over, len(chunks) - 1), *late)
+    return out, failed[0] if checked else None
+
+
+def on_device(tiles, epochs, *args):
+    count, rows, cols = args[0].shape[1:]
+    capacity = max(2, min(count // 2, 64 // epochs))
+    per_dev = PATCHES // epochs
+    cfg = (epochs, capacity, per_dev, tiles, count, rows, cols)
+    full = [
+        (capacity if k == 0 else 0) + (epochs - 1) * size
+        for k, (_, size) in enumerate(plan_chunks(capacity))
+    ]
+    sends = full
+    if capacity >= 16 and tiles == 1 << len(full):
+        sends = [5 * capacity // 4, 7 * capacity // 8, 3 * capacity // 8]
+        sends = [min(a, b) for a, b in zip(sends, full)]
+    out, failed = run(cfg, sends, args)
+    if failed is not None:
+
+        def again(state):
+            return jnp.zeros((), jnp.int32), run(cfg, full, args)[0]
+
+        _, out = lax.while_loop(lambda state: state[0] > 0, again, (failed, out))
     return out.reshape(1, BANDS, per_dev, rows, cols)
 
 
@@ -517,6 +590,10 @@
     )
     out_specs = P("tile", None, "epoch", None, None)
     epochs = mesh.shape["epoch"]
-    device = functools.partial(on_device, mesh.shape["tile"], epochs)
-
-    return jax.shard_map(device, mesh=mesh, in_specs=in_specs, out_specs=out_specs, check_vma=False)
+    return jax.shard_map(
+        functools.partial(on_device, mesh.shape["tile"], epochs),
+        mesh=mesh,
+        in_specs=in_specs,
+        out_specs=out_specs,
+        check_vma=False,
+    )

time: 98.2 us -> 96.5 us (0.983)
  the two profiles are of different devices: /device:TPU:28 before, /device:TPU:1 now
where the time goes in v1:
time: 96.5 us; the launch traced here: 95.2 us
  starting transfers between devices  43.6 us (45%)
  Pallas kernels  26.8 us (28%)
  waiting for transfers between devices  23.7 us (25%)
    ppermute x9, waiting for transfers between devices, turn(): lax.ppermute(x, 'epoch', [(i, (i + d) % epochs) for i in range(epochs)])  21.7 us
    ppermute x9, starting transfers between devices, turn(): lax.ppermute(x, 'epoch', [(i, (i + d) % epochs) for i in range(epochs)])  20.1 us
    ppermute x6, starting transfers between devices, beside(): return lax.ppermute(x, 'tile', route)  18.3 us
    pallas_call x2, Pallas kernels, run(): pl.pallas_call(functools.partial(resample_kernel, cfg, False, chunks[k:k...  10.7 us
    pallas_call x1, Pallas kernels, run(): pl.pallas_call(functools.partial(resample_kernel, cfg, True, chunks[:1],...  7.16 us
    ppermute x3, starting transfers between devices, swap(): return lax.ppermute(x, 'tile', [(i, i ^ 1 << k) for i in range(tiles)])  5.19 us
    pallas_call x3, Pallas kernels, run(): pl.pallas_call(functools.partial(collect_kernel, cfg, queues, k, ends), o...  5.04 us
    pallas_call x1, Pallas kernels, run(): pl.pallas_call(functools.partial(settle_kernel, cfg, queues), out_shape=t...  2.16 us
  transfers between devices with their start and end apart: 18, of which 6 were waited for; matrix products, arithmetic and copies ran while one was open for 0% of the time, Pallas kernels for 18%

profile of v1, /device:TPU:1, one launch (start us, length us, event | category | flops | bytes accessed | tf_op | source)
XLA Modules:
  0.0 95.2 jit_solution(696166320441366305)
XLA Ops:
  0.0 7.2 %resample_0.3 = (f32[264,128]{1,0:T(8,128)S(1)}, f32[264,128]{1,0:T(8,128)S(1)}, f32[264,128]{1,0:T(8,128)S(1)}, bf16[2048,256]{1,0:T(8,128)(2,1)S(1)}, bf16[102...) custom-call(s32[32]{0:T(128)} %bitcast.28, ...), custom_call_target="tpu_custom_call" | custom-call | tf_op jit(solution)/shard_map/resample_0/pallas_call | solution.py:455
  7.2 2.2 %collective-permute-start.15 = (f32[264,128]{1,0:T(8,128)S(1)}, f32[264,128]{1,0:T(8,128)S(1)}, u32[]{:S(2)}, u32[]{:S(2)}) collective-permute-start(f32[264,128]{1,0:T(8,128)S(1)} %get-tuple-element.128), channel_id=1, source_target_pairs={{0,1},{1,2},{2,3},{3,0},{4,5},{5,6},{6,7},{7,4},{8,9},{9,10},{10,1... | collective-permute-start | bytes 405512 | tf_op jit(solution)/shard_map/ppermute | solution.py:482
  9.3 1.8 %shard_map.93 = (f32[520,128]{1,0:T(8,128)S(1)}, f32[520,128]{1,0:T(8,128)S(1)}, f32[520,128]{1,0:T(8,128)S(1)}) custom-call(s32[64]{0:T(128)S(1)} %get-tuple-element.119.refs_0_, s32[64]{0:T(128)S(1)} %get-tuple-element.120.refs_1_, s32[32]{0:T(128)S(1)} %get-tuple-element.121.refs_2_, f32[16,32]{1,0:T(8,128)S(1)} %get-tuple-element.122.refs_3_, ...), custom_call_target="tpu_custom_call" | custom-call | tf_op jit(solution)/shard_map/pallas_call | solution.py:470
  11.2 3.5 %collective-permute-start.18 = (f32[520,128]{1,0:T(8,128)S(1)}, f32[520,128]{1,0:T(8,128)S(1)}, u32[]{:S(2)}, u32[]{:S(2)}) collective-permute-start(f32[520,128]{1,0:T(8,128)S(1)} %get-tuple-element.132), channel_id=1, source_target_pairs={{0,1},{1,2},{2,3},{3,0},{4,5},{5,6},{6,7},{7,4},{8,9},{9,10},{10,1... | collective-permute-start | bytes 798728 | tf_op jit(solution)/shard_map/ppermute | solution.py:482
  14.7 1.1 %collective-permute-start.19 = (f32[520,128]{1,0:T(8,128)S(1)}, f32[520,128]{1,0:T(8,128)S(1)}, u32[]{:S(2)}, u32[]{:S(2)}) collective-permute-start(f32[520,128]{1,0:T(8,128)S(1)} %get-tuple-element.133), channel_id=1, source_target_pairs={{0,2},{1,3},{2,0},{3,1},{4,6},{5,7},{6,4},{7,5},{8,10},{9,11},{10,... | collective-permute-start | bytes 798728 | tf_op jit(solution)/shard_map/ppermute | solution.py:482
  15.8 2.3 %collective-permute-start.20 = (f32[520,128]{1,0:T(8,128)S(1)}, f32[520,128]{1,0:T(8,128)S(1)}, u32[]{:S(2)}, u32[]{:S(2)}) collective-permute-start(f32[520,128]{1,0:T(8,128)S(1)} %get-tuple-element.134), channel_id=1, source_target_pairs={{0,3},{1,0},{2,1},{3,2},{4,7},{5,4},{6,5},{7,6},{8,11},{9,8},{10,9... | collective-permute-start | bytes 798728 | tf_op jit(solution)/shard_map/ppermute | solution.py:482
  18.1 1.3 %collective-permute-start.17 = (f32[264,128]{1,0:T(8,128)S(1)}, f32[264,128]{1,0:T(8,128)S(1)}, u32[]{:S(2)}, u32[]{:S(2)}) collective-permute-start(f32[264,128]{1,0:T(8,128)S(1)} %get-tuple-element.130), channel_id=1, source_target_pairs={{0,3},{1,0},{2,1},{3,2},{4,7},{5,4},{6,5},{7,6},{8,11},{9,8},{10,9... | collective-permute-start | bytes 405512 | tf_op jit(solution)/shard_map/ppermute | solution.py:482
  19.3 8.9 %shard_map.91 = (f32[264,128]{1,0:T(8,128)S(1)}, f32[264,128]{1,0:T(8,128)S(1)}, f32[264,128]{1,0:T(8,128)S(1)}, f32[1032,128]{1,0:T(8,128)S(1)}) custom-call(s32[64]{0:T(128)S(1)} %get-tuple-element.119.refs_0_, s32[64]{0:T(128)S(1)} %get-tuple-element.120.refs_1_, s32[32]{0:T(128)S(1)} %get-tuple-element.121.refs_2_, ...), custom_call_target="tpu_custom_call" | custom-call | tf_op jit(solution)/shard_map/pallas_call | solution.py:470
  28.2 17.2 %collective-permute-done.16.refs_2_.refs_5_.refs_3_ = f32[264,128]{1,0:T(8,128)S(1)} collective-permute-done((f32[264,128]{1,0:T(8,128)S(1)}, f32[264,128]{1,0:T(8,128)S(1)}, u32[]{:S(2)}, u32[]{:S(2)}) %collective-permute-start.16) | collective-permute-done | bytes 135200 | tf_op jit(solution)/shard_map/ppermute | solution.py:482
  45.4 3.1 %shard_map.92 = (f32[1288,128]{1,0:T(8,128)S(1)}, f32[1288,128]{1,0:T(8,128)S(1)}, s32[235]{0:T(256)S(1)}, f32[8,128]{1,0:T(8,128)S(1)}) custom-call(f32[1032,128]{1,0:T(8,128)S(1)} %get-tuple-element.127.refs_0_.refs_3_.refs_1_, f32[264,128]{1,0:T(8,128)S(1)} %collective-permute-done.15.refs_1_.refs_4_.refs_2_, ...), custom_call_target="tpu_custom_call" | custom-call | tf_op jit(solution)/shard_map/pallas_call | solution.py:509
  48.5 0.3 collective-permute-start.26
  48.8 0.9 collective-permute-done.26.refs_2_
  49.8 1.1 %shard_map.94 = (f32[904,128]{1,0:T(8,128)S(1)}, f32[904,128]{1,0:T(8,128)S(1)}, f32[8,128]{1,0:T(8,128)S(1)}) custom-call(s32[235]{0:T(256)S(1)} %get-tuple-element.131.refs_0_, f32[8,128]{1,0:T(8,128)S(1)} %get-tuple-element.140.refs_1_, f32[8,128]{1,0:T(8,128)S(1)} %collective-permute-done.26.refs_2_, ...), custom_call_target="tpu_custom_call" | custom-call | tf_op jit(solution)/shard_map/pallas_call | solution.py:509
  50.9 1.9 %collective-permute-start.27 = (f32[904,128]{1,0:T(8,128)S(1)}, f32[904,128]{1,0:T(8,128)S(1)}, u32[]{:S(2)}, u32[]{:S(2)}) collective-permute-start(f32[904,128]{1,0:T(8,128)S(1)} %get-tuple-element.141), channel_id=1, source_target_pairs={{4,0},{8,4},{12,8},{16,12},{20,16},{24,20},{28,24},{5,1},{9,5},{13... | collective-permute-start | bytes 1388552 | tf_op jit(solution)/shard_map/ppermute | solution.py:486
  52.8 1.9 %collective-permute-start.24 = (f32[1288,128]{1,0:T(8,128)S(1)}, f32[1288,128]{1,0:T(8,128)S(1)}, u32[]{:S(2)}, u32[]{:S(2)}) collective-permute-start(f32[1288,128]{1,0:T(8,128)S(1)} %get-tuple-element.138), channel_id=1, source_target_pairs={{4,0},{8,4},{12,8},{16,12},{20,16},{24,20},{28,24},{5,1},{9,5},{13... | collective-permute-start | bytes 1978376 | tf_op jit(solution)/shard_map/ppermute | solution.py:486
  54.8 3.6 %collective-permute-start.25 = (f32[1288,128]{1,0:T(8,128)S(1)}, f32[1288,128]{1,0:T(8,128)S(1)}, u32[]{:S(2)}, u32[]{:S(2)}) collective-permute-start(f32[1288,128]{1,0:T(8,128)S(1)} %get-tuple-element.139), channel_id=1, source_target_pairs={{0,4},{4,8},{8,12},{12,16},{16,20},{20,24},{24,28},{1,5},{5,9},{9,... | collective-permute-start | bytes 1978376 | tf_op jit(solution)/shard_map/ppermute | solution.py:486
  58.4 3.3 %collective-permute-start.21 = (f32[264,128]{1,0:T(8,128)S(1)}, f32[264,128]{1,0:T(8,128)S(1)}, u32[]{:S(2)}, u32[]{:S(2)}) collective-permute-start(f32[264,128]{1,0:T(8,128)S(1)} %get-tuple-element.135), channel_id=1, source_target_pairs={{0,1},{1,2},{2,3},{3,0},{4,5},{5,6},{6,7},{7,4},{8,9},{9,10},{10,1... | collective-permute-start | bytes 405512 | tf_op jit(solution)/shard_map/ppermute | solution.py:482
  61.7 3.3 %collective-permute-start.22 = (f32[264,128]{1,0:T(8,128)S(1)}, f32[264,128]{1,0:T(8,128)S(1)}, u32[]{:S(2)}, u32[]{:S(2)}) collective-permute-start(f32[264,128]{1,0:T(8,128)S(1)} %get-tuple-element.136), channel_id=1, source_target_pairs={{0,2},{1,3},{2,0},{3,1},{4,6},{5,7},{6,4},{7,5},{8,10},{9,11},{10,... | collective-permute-start | bytes 405512 | tf_op jit(solution)/shard_map/ppermute | solution.py:482
  65.0 2.2 %collective-permute-done.21.refs_8_.refs_10_ = f32[264,128]{1,0:T(8,128)S(1)} collective-permute-done((f32[264,128]{1,0:T(8,128)S(1)}, f32[264,128]{1,0:T(8,128)S(1)}, u32[]{:S(2)}, u32[]{:S(2)}) %collective-permute-start.21) | collective-permute-done | bytes 135200 | tf_op jit(solution)/shard_map/ppermute | solution.py:482
  67.2 3.3 %collective-permute-start.28 = (f32[904,128]{1,0:T(8,128)S(1)}, f32[904,128]{1,0:T(8,128)S(1)}, u32[]{:S(2)}, u32[]{:S(2)}) collective-permute-start(f32[904,128]{1,0:T(8,128)S(1)} %get-tuple-element.142), channel_id=1, source_target_pairs={{0,4},{4,8},{8,12},{12,16},{16,20},{20,24},{24,28},{1,5},{5,9},{9,... | collective-permute-start | bytes 1388552 | tf_op jit(solution)/shard_map/ppermute | solution.py:486
  70.5 0.3 collective-permute-done.22.refs_9_.refs_11_
  70.8 3.2 %collective-permute-start.23 = (f32[264,128]{1,0:T(8,128)S(1)}, f32[264,128]{1,0:T(8,128)S(1)}, u32[]{:S(2)}, u32[]{:S(2)}) collective-permute-start(f32[264,128]{1,0:T(8,128)S(1)} %get-tuple-element.137), channel_id=1, source_target_pairs={{0,3},{1,0},{2,1},{3,2},{4,7},{5,4},{6,5},{7,6},{8,11},{9,8},{10,9... | collective-permute-start | bytes 405512 | tf_op jit(solution)/shard_map/ppermute | solution.py:482
  74.0 2.0 %collective-permute-done.23.refs_10_.refs_12_ = f32[264,128]{1,0:T(8,128)S(1)} collective-permute-done((f32[264,128]{1,0:T(8,128)S(1)}, f32[264,128]{1,0:T(8,128)S(1)}, u32[]{:S(2)}, u32[]{:S(2)}) %collective-permute-start.23) | collective-permute-done | bytes 135200 | tf_op jit(solution)/shard_map/ppermute | solution.py:482
  76.0 4.1 %collective-permute-start.29 = (f32[8,128]{1,0:T(8,128)S(1)}, f32[8,128]{1,0:T(8,128)S(1)}, u32[]{:S(2)}, u32[]{:S(2)}) collective-permute-start(f32[8,128]{1,0:T(8,128)S(1)} %get-tuple-element.143.refs_1_), channel_id=1, source_target_pairs={{0,8},{4,12},{8,0},{12,4},{16,24},{20,28},{24,16},{28,20},{1,9},{5... | collective-permute-start | bytes 12296 | tf_op jit(solution)/shard_map/ppermute | solution.py:491
  80.1 1.0 %collective-permute-done.29.refs_2_ = f32[8,128]{1,0:T(8,128)S(1)} collective-permute-done((f32[8,128]{1,0:T(8,128)S(1)}, f32[8,128]{1,0:T(8,128)S(1)}, u32[]{:S(2)}, u32[]{:S(2)}) %collective-permute-start.29) | collective-permute-done | bytes 4128 | tf_op jit(solution)/shard_map/ppermute | solution.py:491
  81.1 0.8 shard_map.95
  81.9 4.0 %collective-permute-start.31 = (f32[392,128]{1,0:T(8,128)S(1)}, f32[392,128]{1,0:T(8,128)S(1)}, u32[]{:S(2)}, u32[]{:S(2)}) collective-permute-start(f32[392,128]{1,0:T(8,128)S(1)} %get-tuple-element.145), channel_id=1, source_target_pairs={{4,0},{8,4},{12,8},{16,12},{20,16},{24,20},{28,24},{5,1},{9,5},{13... | collective-permute-start | bytes 602120 | tf_op jit(solution)/shard_map/ppermute | solution.py:486
  85.9 3.5 %collective-permute-start.32 = (f32[392,128]{1,0:T(8,128)S(1)}, f32[392,128]{1,0:T(8,128)S(1)}, u32[]{:S(2)}, u32[]{:S(2)}) collective-permute-start(f32[392,128]{1,0:T(8,128)S(1)} %get-tuple-element.146), channel_id=1, source_target_pairs={{0,4},{4,8},{8,12},{12,16},{16,20},{20,24},{24,28},{1,5},{5,9},{9,... | collective-permute-start | bytes 602120 | tf_op jit(solution)/shard_map/ppermute | solution.py:486
  89.5 0.8 collective-permute-start.30
  90.3 2.2 %settle.3.refs_0_ = f32[48,64,128]{2,1,0:T(8,128)S(1)} custom-call(s32[235]{0:T(256)S(1)} %get-tuple-element.131.refs_0_, f32[1032,128]{1,0:T(8,128)S(1)} %get-tuple-element.127.refs_0_.refs_3_.refs_1_, f32[264,128]{1,0:T(8,128)S(1)} %collective-permute-done.15.refs_1_.refs_4_.refs_2_, f32[264,128]{1,0:T(8,128)S(1)} %collective-permute-done.16.refs_2_.refs_5_.refs_3_, ...), custom_call_target="tpu_custom_call" | custom-call | tf_op jit(solution)/shard_map/settle/pallas_call | solution.py:530
  92.5 1.8 %finish.3 = (f32[48,64,128]{2,1,0:T(8,128)}, s32[1]{0:T(128)}) custom-call(f32[48,64,128]{2,1,0:T(8,128)S(1)} %settle.3.refs_0_, f32[8,128]{1,0:T(8,128)S(1)} %get-tuple-element.144.refs_1_, f32[8,128]{1,0:T(8,128)S(1)} %collective-permute-done.30.refs_2_, f32[392,128]{1,0:T(8,128)S(1)} %collective-permute-done.31.refs_3_, ...), custom_call_target="tpu_custom_call" | custom-call | tf_op jit(solution)/shard_map/finish/pallas_call | solution.py:539
  94.2 0.8 while.9
  (13 shorter events, 0.0 us)
Async XLA Ops:
  7.2 10.9 %collective-permute-start.15 = (f32[264,128]{1,0:T(8,128)S(1)}, f32[264,128]{1,0:T(8,128)S(1)}, u32[]{:S(2)}, u32[]{:S(2)}) collective-permute-start(f32[264,128]{1,0:T(8,128)S(1)} %get-tuple-element.128), channel_id=1, source_target_pairs={{0,1},{1,2},{2,3},{3,0},{4,5},{5,6},{6,7},{7,4},{8,9},{9,10},{10,1... | collective-permute-start | bytes 405512 | tf_op jit(solution)/shard_map/ppermute | solution.py:482
  11.2 38.6 %collective-permute-start.18 = (f32[520,128]{1,0:T(8,128)S(1)}, f32[520,128]{1,0:T(8,128)S(1)}, u32[]{:S(2)}, u32[]{:S(2)}) collective-permute-start(f32[520,128]{1,0:T(8,128)S(1)} %get-tuple-element.132), channel_id=1, source_target_pairs={{0,1},{1,2},{2,3},{3,0},{4,5},{5,6},{6,7},{7,4},{8,9},{9,10},{10,1... | collective-permute-start | bytes 798728 | tf_op jit(solution)/shard_map/ppermute | solution.py:482
  14.7 35.1 %collective-permute-start.19 = (f32[520,128]{1,0:T(8,128)S(1)}, f32[520,128]{1,0:T(8,128)S(1)}, u32[]{:S(2)}, u32[]{:S(2)}) collective-permute-start(f32[520,128]{1,0:T(8,128)S(1)} %get-tuple-element.133), channel_id=1, source_target_pairs={{0,2},{1,3},{2,0},{3,1},{4,6},{5,7},{6,4},{7,5},{8,10},{9,11},{10,... | collective-permute-start | bytes 798728 | tf_op jit(solution)/shard_map/ppermute | solution.py:482
  15.8 34.0 %collective-permute-start.20 = (f32[520,128]{1,0:T(8,128)S(1)}, f32[520,128]{1,0:T(8,128)S(1)}, u32[]{:S(2)}, u32[]{:S(2)}) collective-permute-start(f32[520,128]{1,0:T(8,128)S(1)} %get-tuple-element.134), channel_id=1, source_target_pairs={{0,3},{1,0},{2,1},{3,2},{4,7},{5,4},{6,5},{7,6},{8,11},{9,8},{10,9... | collective-permute-start | bytes 798728 | tf_op jit(solution)/shard_map/ppermute | solution.py:482
  18.1 27.3 %collective-permute-start.16 = (f32[264,128]{1,0:T(8,128)S(1)}, f32[264,128]{1,0:T(8,128)S(1)}, u32[]{:S(2)}, u32[]{:S(2)}) collective-permute-start(f32[264,128]{1,0:T(8,128)S(1)} %get-tuple-element.129), channel_id=1, source_target_pairs={{0,2},{1,3},{2,0},{3,1},{4,6},{5,7},{6,4},{7,5},{8,10},{9,11},{10,... | collective-permute-start | bytes 405512 | tf_op jit(solution)/shard_map/ppermute | solution.py:482
  18.1 27.3 %collective-permute-start.17 = (f32[264,128]{1,0:T(8,128)S(1)}, f32[264,128]{1,0:T(8,128)S(1)}, u32[]{:S(2)}, u32[]{:S(2)}) collective-permute-start(f32[264,128]{1,0:T(8,128)S(1)} %get-tuple-element.130), channel_id=1, source_target_pairs={{0,3},{1,0},{2,1},{3,2},{4,7},{5,4},{6,5},{7,6},{8,11},{9,8},{10,9... | collective-permute-start | bytes 405512 | tf_op jit(solution)/shard_map/ppermute | solution.py:482
  48.5 1.2 %collective-permute-start.26 = (f32[8,128]{1,0:T(8,128)S(1)}, f32[8,128]{1,0:T(8,128)S(1)}, u32[]{:S(2)}, u32[]{:S(2)}) collective-permute-start(f32[8,128]{1,0:T(8,128)S(1)} %get-tuple-element.140.refs_1_), channel_id=1, source_target_pairs={{0,4},{4,0},{8,12},{12,8},{16,20},{20,16},{24,28},{28,24},{1,5},{5... | collective-permute-start | bytes 12296 | tf_op jit(solution)/shard_map/ppermute | solution.py:491
  50.9 35.0 %collective-permute-start.27 = (f32[904,128]{1,0:T(8,128)S(1)}, f32[904,128]{1,0:T(8,128)S(1)}, u32[]{:S(2)}, u32[]{:S(2)}) collective-permute-start(f32[904,128]{1,0:T(8,128)S(1)} %get-tuple-element.141), channel_id=1, source_target_pairs={{4,0},{8,4},{12,8},{16,12},{20,16},{24,20},{28,24},{5,1},{9,5},{13... | collective-permute-start | bytes 1388552 | tf_op jit(solution)/shard_map/ppermute | solution.py:486
  52.8 37.4 %collective-permute-start.24 = (f32[1288,128]{1,0:T(8,128)S(1)}, f32[1288,128]{1,0:T(8,128)S(1)}, u32[]{:S(2)}, u32[]{:S(2)}) collective-permute-start(f32[1288,128]{1,0:T(8,128)S(1)} %get-tuple-element.138), channel_id=1, source_target_pairs={{4,0},{8,4},{12,8},{16,12},{20,16},{24,20},{28,24},{5,1},{9,5},{13... | collective-permute-start | bytes 1978376 | tf_op jit(solution)/shard_map/ppermute | solution.py:486
  54.8 35.5 %collective-permute-start.25 = (f32[1288,128]{1,0:T(8,128)S(1)}, f32[1288,128]{1,0:T(8,128)S(1)}, u32[]{:S(2)}, u32[]{:S(2)}) collective-permute-start(f32[1288,128]{1,0:T(8,128)S(1)} %get-tuple-element.139), channel_id=1, source_target_pairs={{0,4},{4,8},{8,12},{12,16},{16,20},{20,24},{24,28},{1,5},{5,9},{9,... | collective-permute-start | bytes 1978376 | tf_op jit(solution)/shard_map/ppermute | solution.py:486
  58.4 8.8 %collective-permute-start.21 = (f32[264,128]{1,0:T(8,128)S(1)}, f32[264,128]{1,0:T(8,128)S(1)}, u32[]{:S(2)}, u32[]{:S(2)}) collective-permute-start(f32[264,128]{1,0:T(8,128)S(1)} %get-tuple-element.135), channel_id=1, source_target_pairs={{0,1},{1,2},{2,3},{3,0},{4,5},{5,6},{6,7},{7,4},{8,9},{9,10},{10,1... | collective-permute-start | bytes 405512 | tf_op jit(solution)/shard_map/ppermute | solution.py:482
  61.7 9.1 %collective-permute-start.22 = (f32[264,128]{1,0:T(8,128)S(1)}, f32[264,128]{1,0:T(8,128)S(1)}, u32[]{:S(2)}, u32[]{:S(2)}) collective-permute-start(f32[264,128]{1,0:T(8,128)S(1)} %get-tuple-element.136), channel_id=1, source_target_pairs={{0,2},{1,3},{2,0},{3,1},{4,6},{5,7},{6,4},{7,5},{8,10},{9,11},{10,... | collective-permute-start | bytes 405512 | tf_op jit(solution)/shard_map/ppermute | solution.py:482
  67.2 22.2 %collective-permute-start.28 = (f32[904,128]{1,0:T(8,128)S(1)}, f32[904,128]{1,0:T(8,128)S(1)}, u32[]{:S(2)}, u32[]{:S(2)}) collective-permute-start(f32[904,128]{1,0:T(8,128)S(1)} %get-tuple-element.142), channel_id=1, source_target_pairs={{0,4},{4,8},{8,12},{12,16},{16,20},{20,24},{24,28},{1,5},{5,9},{9,... | collective-permute-start | bytes 1388552 | tf_op jit(solution)/shard_map/ppermute | solution.py:486
  70.8 5.2 %collective-permute-start.23 = (f32[264,128]{1,0:T(8,128)S(1)}, f32[264,128]{1,0:T(8,128)S(1)}, u32[]{:S(2)}, u32[]{:S(2)}) collective-permute-start(f32[264,128]{1,0:T(8,128)S(1)} %get-tuple-element.137), channel_id=1, source_target_pairs={{0,3},{1,0},{2,1},{3,2},{4,7},{5,4},{6,5},{7,6},{8,11},{9,8},{10,9... | collective-permute-start | bytes 405512 | tf_op jit(solution)/shard_map/ppermute | solution.py:482
  76.0 5.1 %collective-permute-start.29 = (f32[8,128]{1,0:T(8,128)S(1)}, f32[8,128]{1,0:T(8,128)S(1)}, u32[]{:S(2)}, u32[]{:S(2)}) collective-permute-start(f32[8,128]{1,0:T(8,128)S(1)} %get-tuple-element.143.refs_1_), channel_id=1, source_target_pairs={{0,8},{4,12},{8,0},{12,4},{16,24},{20,28},{24,16},{28,20},{1,9},{5... | collective-permute-start | bytes 12296 | tf_op jit(solution)/shard_map/ppermute | solution.py:491
  81.9 10.6 %collective-permute-start.31 = (f32[392,128]{1,0:T(8,128)S(1)}, f32[392,128]{1,0:T(8,128)S(1)}, u32[]{:S(2)}, u32[]{:S(2)}) collective-permute-start(f32[392,128]{1,0:T(8,128)S(1)} %get-tuple-element.145), channel_id=1, source_target_pairs={{4,0},{8,4},{12,8},{16,12},{20,16},{24,20},{28,24},{5,1},{9,5},{13... | collective-permute-start | bytes 602120 | tf_op jit(solution)/shard_map/ppermute | solution.py:486
  85.9 6.5 %collective-permute-start.32 = (f32[392,128]{1,0:T(8,128)S(1)}, f32[392,128]{1,0:T(8,128)S(1)}, u32[]{:S(2)}, u32[]{:S(2)}) collective-permute-start(f32[392,128]{1,0:T(8,128)S(1)} %get-tuple-element.146), channel_id=1, source_target_pairs={{0,4},{4,8},{8,12},{12,16},{16,20},{20,24},{24,28},{1,5},{5,9},{9,... | collective-permute-start | bytes 602120 | tf_op jit(solution)/shard_map/ppermute | solution.py:486
  89.5 3.0 %collective-permute-start.30 = (f32[8,128]{1,0:T(8,128)S(1)}, f32[8,128]{1,0:T(8,128)S(1)}, u32[]{:S(2)}, u32[]{:S(2)}) collective-permute-start(f32[8,128]{1,0:T(8,128)S(1)} %get-tuple-element.144.refs_1_), channel_id=1, source_target_pairs={{0,16},{4,20},{8,24},{12,28},{16,0},{20,4},{24,8},{28,12},{1,17},{... | collective-permute-start | bytes 12296 | tf_op jit(solution)/shard_map/ppermute | solution.py:491
